TPU v7x, 256 devices: a whole 4x4x8 slice. The times are simulated.
256 devices in a mesh: seq: 64 (over x, z, core), ch: 4 (over y).
Axes of the slice: x: 4, y: 4, z: 8, core: 2. Of those that a mesh axis runs over, the one named last changes fastest.
Arguments:
- gate_rows: bfloat16 [32768, 2048], P(('seq', 'ch')), may hold values from -6 to 6
- key_rows: bfloat16 [32768, 2048], P(('seq', 'ch')), may hold values from -6 to 6
- value_rows: bfloat16 [32768, 2048], P(('seq', 'ch')), may hold values from -6 to 6
- spectrum: float32 [2, 128, 512, 2048], P(None, 'seq', None, 'ch'), may hold values from -6 to 6
- skip_bias: float32 [2048], replicated, may hold values from -1 to 1
Outputs:
- gated: bfloat16 [32768, 2048], P(('seq', 'ch'))
All inputs are finite; a program needn't handle non-finite values.
Results may differ from a plain program's by a relative error of at most 0.0049.
Values may be sent and summed in bfloat16 or wider, within the bound.
A program may use at most 128 MiB of HBM per device.

v0:
```python
import math
import jax
import jax.numpy as jnp
import numpy as np
from jax import lax
from jax.sharding import PartitionSpec as P

f32, bf16 = (jnp.float32, jnp.bfloat16)


def phase_table(first, second, modulus):
    turns = first[:, None] * second[None, :] % modulus
    angles = turns.astype(f32) * (2.0 * math.pi / modulus)
    return (jnp.cos(angles), jnp.sin(angles))


def dot(eq, a, b):
    return jnp.einsum(eq, a.astype(bf16), b.astype(bf16), preferred_element_type=f32)


def convolve(product, spectrum):
    seq_count = lax.axis_size("seq")
    tokens, width = product.shape
    length_two = 2 * seq_count * tokens
    offsets = jnp.arange(2 * seq_count, dtype=jnp.int32)
    places = jnp.arange(seq_count, dtype=jnp.int32)
    residues = jnp.arange(tokens, dtype=jnp.int32)
    off_cos, off_sin = phase_table(offsets, places, 2 * seq_count)
    res_cos, res_sin = phase_table(residues, residues, tokens)
    block = tokens // seq_count
    device = lax.axis_index("seq")
    values = lax.all_to_all(
        product.reshape(1, tokens, width), "seq", split_axis=1, concat_axis=0, tiled=True
    )
    off = jnp.stack([off_cos, -off_sin], 1)
    part = dot("kip,prc->kirc", off, values)
    own_rows = device * block + jnp.arange(block, dtype=jnp.int32)
    tw_cos, tw_sin = phase_table(offsets, own_rows, length_two)
    tw_cos = tw_cos[:, :, None]
    tw_sin = tw_sin[:, :, None]
    part = jnp.stack(
        [part[:, 0] * tw_cos + part[:, 1] * tw_sin, part[:, 1] * tw_cos - part[:, 0] * tw_sin], 1
    )
    part = lax.all_to_all(part.astype(bf16), "seq", split_axis=0, concat_axis=2, tiled=True)
    table = jnp.stack([jnp.stack([res_cos, res_sin], 0), jnp.stack([-res_sin, res_cos], 0)], 0)
    nxt = dot("oisr,girc->gosc", table, part)
    re, im = (nxt[:, 0], nxt[:, 1])
    spec_real, spec_imag = (spectrum[0], spectrum[1])
    filt = jnp.stack([re * spec_real - im * spec_imag, re * spec_imag + im * spec_real], 1)
    back = dot("oisr,gosc->girc", table, filt)
    own_offsets = 2 * device + jnp.arange(2, dtype=jnp.int32)
    un_cos, un_sin = phase_table(own_offsets, residues, length_two)
    un_cos = un_cos[:, :, None]
    un_sin = un_sin[:, :, None]
    back = jnp.stack(
        [back[:, 0] * un_cos - back[:, 1] * un_sin, back[:, 1] * un_cos + back[:, 0] * un_sin], 1
    )
    back = lax.all_to_all(back.astype(bf16), "seq", split_axis=2, concat_axis=0, tiled=True)
    field = dot("kip,kirc->prc", off, back) / length_two
    field = lax.all_to_all(field.astype(bf16), "seq", split_axis=0, concat_axis=1, tiled=True)
    return field.reshape(tokens, width)


def per_device(gate_rows, key_rows, value_rows, spectrum, skip_bias):
    product = (key_rows.astype(f32) * value_rows.astype(f32)).astype(bf16)
    cols = lax.all_to_all(product, "ch", split_axis=1, concat_axis=0, tiled=True)
    field = convolve(cols, spectrum)
    field = lax.all_to_all(field, "ch", split_axis=0, concat_axis=1, tiled=True)
    gated = gate_rows.astype(f32) * (field.astype(f32) + skip_bias[None, :] * product.astype(f32))
    return gated.astype(bf16)


def solution(mesh):
    placed = (
        P(("seq", "ch"), None),
        P(("seq", "ch"), None),
        P(("seq", "ch"), None),
        P(None, "seq", None, "ch"),
        P(),
    )
    return jax.shard_map(
        per_device, mesh=mesh, in_specs=placed, out_specs=P(("seq", "ch"), None), check_vma=False
    )
```

profile of v0, /device:TPU:1, one launch (start us, length us, event | category | flops | bytes accessed | tf_op | source)
XLA Modules:
  0.0 231.2 jit_solution(8587661304348707398)
XLA Ops:
  0.0 1.3 copy.53
  1.3 1.3 copy.54
  2.8 13.4 %all_to_all.86 = bf16[128,4,512]{0,2,1:T(8,128)(2,1)S(1)} all-to-all(bf16[128,4,512]{0,2,1:T(8,128)(2,1)S(1)} %bitcast.98), channel_id=1, replica_groups=mesh['seq'=64,'ch'=4] {'ch'}, dimensions={1} | all-to-all | bytes 1048576 | tf_op jit(solution)/shard_map/all_to_all | solution.py:66
  16.4 0.8 copy.98
  17.7 3.8 %reduce = bf16[512,512]{1,0:T(8,128)(2,1)S(1)} reduce(bf16[512,1,512]{2,1,0:T(2,128)(2,1)S(1)} %bitcast.100, bf16[]{:T(256)} %broadcast.368), dimensions={1}, to_apply=%bitcast.96.reduce_sub_computation | reduce | bytes 1048578
  21.5 1.0 reshape.296
  22.5 13.3 %all-to-all-start.1 = ((bf16[64,2,2048]{2,1,0:T(2,128)(2,1)}), bf16[64,2,2048]{2,1,0:T(2,128)(2,1)S(1)}, u32[]{:S(2)}, u32[]{:S(2)}) async-start(bf16[64,2,2048]{2,1,0:T(2,128)(2,1)} %reshape.296), calls=%async_computation.1 | async-start | bytes 1048576 | tf_op jit(solution)/shard_map/all_to_all | solution.py:32
  36.2 17.0 %all-to-all-done.1 = bf16[64,2,2048]{2,1,0:T(2,128)(2,1)S(1)} async-done(((bf16[64,2,2048]{2,1,0:T(2,128)(2,1)}), bf16[64,2,2048]{2,1,0:T(2,128)(2,1)S(1)}, u32[]{:S(2)}, u32[]{:S(2)}) %all-to-all-start.1) | async-done | bytes 524320 | tf_op jit(solution)/shard_map/all_to_all | solution.py:32
  53.2 0.5 reshape.297
  53.9 0.7 fusion.21
  54.6 0.6 add_convert_fusion.1
  55.4 2.5 %copy.58 = bf16[128,2,8,512]{3,2,1,0:T(8,128)(2,1)} copy(bf16[128,2,8,512]{3,0,2,1:T(8,128)(2,1)S(1)} %pad_maximum_fusion) | data formatting | bytes 4194304 | tf_op jit(solution)/shard_map/stack | solution.py:41
  57.9 6.5 %all-to-all-start.2 = ((bf16[128,2,8,512]{3,2,1,0:T(8,128)(2,1)}), bf16[128,2,8,512]{3,2,1,0:T(8,128)(2,1)}, u32[]{:S(2)}, u32[]{:S(2)}) async-start(bf16[128,2,8,512]{3,2,1,0:T(8,128)(2,1)} %copy.58), calls=%async_computation.2 | async-start | bytes 4194304 | tf_op jit(solution)/shard_map/all_to_all | solution.py:44
  64.4 4.6 %fusion.50 = (f32[1,2,512,512]{3,2,1,0:T(8,128)}, f32[1,2,512,512]{3,2,1,0:T(8,128)}) fusion(f32[2,2,512,512]{3,2,1,0:T(8,128)} %param.8), kind=kLoop, calls=%fused_computation.91 | loop fusion | bytes 8388608 | tf_op jit(solution)/shard_map/slice | solution.py:48
  69.0 1.9 copy.79
  71.0 2.9 %copy.80 = f32[1,2,512,512]{2,3,1,0:T(8,128)} copy(f32[1,2,512,512]{3,2,1,0:T(8,128)} %get-tuple-element.12) | data formatting | bytes 4194304
  73.9 4.0 %fusion.25 = bf16[1,512,512]{2,1,0:T(8,128)(2,1)S(1)} fusion(), kind=kLoop, calls=%fused_computation.52 | loop fusion | flops 3932160 | bytes 524288 | tf_op jit(solution)/shard_map/convert.13
  77.8 4.3 %negate_convert_fusion = (bf16[1,512,512]{2,1,0:T(8,128)(2,1)S(1)}, bf16[1,512,512]{2,1,0:T(8,128)(2,1)S(1)}) fusion(), kind=kLoop, calls=%fused_computation.41 | loop fusion | flops 4456448 | bytes 1048576 | tf_op jit(solution)/shard_map/convert.9
  82.2 1.5 maximum_bitcast_fusion.2
  83.9 31.6 %all-to-all-done.2 = bf16[128,2,8,512]{3,2,1,0:T(8,128)(2,1)} async-done(((bf16[128,2,8,512]{3,2,1,0:T(8,128)(2,1)}), bf16[128,2,8,512]{3,2,1,0:T(8,128)(2,1)}, u32[]{:S(2)}, u32[]{:S(2)}) %all-to-all-start.2) | async-done | bytes 2097184 | tf_op jit(solution)/shard_map/all_to_all | solution.py:44
  115.5 4.7 %convolution_bitcast_fusion.1 = f32[2,2,512,512]{2,3,1,0:T(8,128)S(1)} fusion(bf16[2,2,64,8,512]{4,3,1,0,2:T(8,128)(2,1)} %bitcast.7, bf16[1,2,512,512]{3,2,1,0:T(8,128)(2,1)} %get-tuple-element.14, bf16[1,2,512,512]{3,2,1,0:T(8,128)(2,1)} %get-tuple-element.13), kind=kOutput, calls=%fused_computation.1 | convolution fusion | flops 2151677952 | bytes 8388608 | tf_op jit(solution)/shard_map/oisr,girc->gosc/dot_general | solution.py:18
  120.3 1.2 fusion.5
  121.8 2.3 %convolution_bitcast_fusion = f32[2,2,512,512]{2,3,1,0:T(8,128)S(1)} fusion(bf16[2,1,512,512]{2,3,1,0:T(8,128)(2,1)S(1)} %get-tuple-element.6, bf16[2,1,512,512]{2,3,1,0:T(8,128)(2,1)S(1)} %get-tuple-element.5, bf16[1,2,512,512]{3,2,1,0:T(8,128)(2,1)S(1)} %copy-done.2, bf16[1,2,512,512]{3,2,1,0:T(8,128)(2,1)S(1)} %copy-done.1), kind=kOutput, calls=%fused_computation | convolution fusion | flops 2152726528 | bytes 8388608 | tf_op jit(solution)/shard_map/oisr,gosc->girc/dot_general | solution.py:18
  124.1 0.7 subtract_convert_fusion
  125.0 4.0 %copy.64 = bf16[2,2,512,512]{3,1,0,2:T(2,128)(2,1)} copy(bf16[2,2,512,512]{2,3,1,0:T(8,128)(2,1)S(1)} %pad_maximum_fusion.2) | data formatting | bytes 4194304 | tf_op jit(solution)/shard_map/stack | solution.py:55
  129.1 57.1 %all_to_all.87 = bf16[2,2,512,512]{3,1,0,2:T(2,128)(2,1)S(1)} all-to-all(bf16[2,2,512,512]{3,1,0,2:T(2,128)(2,1)} %copy.64), channel_id=1, replica_groups=mesh['seq'=64,'ch'=4] {'seq'}, dimensions={2} | all-to-all | bytes 4194304 | tf_op jit(solution)/shard_map/all_to_all | solution.py:58
  186.6 3.5 %copy.66 = bf16[64,2,2,8,512]{4,1,0,2,3:T(2,128)(2,1)} copy(bf16[64,2,2,8,512]{4,3,0,2,1:T(8,128)(2,1)S(1)} %bitcast.97) | data formatting | bytes 4194304 | tf_op jit(solution)/shard_map/all_to_all | solution.py:58
  190.1 2.7 %all_to_all.76 = bf16[128,2,8,512]{3,0,1,2:T(8,128)(2,1)S(1)} reshape(bf16[64,2,2,8,512]{4,1,0,2,3:T(2,128)(2,1)} %copy.66) | data formatting | bytes 4194304 | tf_op jit(solution)/shard_map/all_to_all | solution.py:58
  193.6 23.0 %all_to_all.88 = bf16[64,8,512]{2,1,0:T(8,128)(2,1)} all-to-all(bf16[64,8,512]{2,1,0:T(8,128)(2,1)S(1)} %copy.67), channel_id=1, replica_groups=mesh['seq'=64,'ch'=4] {'seq'}, dimensions={0} | all-to-all | bytes 1048576 | tf_op jit(solution)/shard_map/all_to_all | solution.py:60
  216.7 3.5 %all-to-all-start.5 = ((bf16[4,128,512]{2,1,0:T(8,128)(2,1)}), bf16[4,128,512]{2,1,0:T(8,128)(2,1)S(1)}, u32[]{:S(2)}, u32[]{:S(2)}) async-start(bf16[4,128,512]{2,1,0:T(8,128)(2,1)} %bitcast.30), calls=%async_computation.5 | async-start | bytes 1048576 | tf_op jit(solution)/shard_map/all_to_all | solution.py:68
  220.4 9.0 %all-to-all-done.5 = bf16[4,128,512]{2,1,0:T(8,128)(2,1)S(1)} async-done(((bf16[4,128,512]{2,1,0:T(8,128)(2,1)}), bf16[4,128,512]{2,1,0:T(8,128)(2,1)S(1)}, u32[]{:S(2)}, u32[]{:S(2)}) %all-to-all-start.5) | async-done | bytes 524320 | tf_op jit(solution)/shard_map/all_to_all | solution.py:68
  230.2 1.0 copy.69
  (28 shorter events, 4.4 us)
Async XLA Ops:
  22.5 30.7 %all-to-all-start.1 = ((bf16[64,2,2048]{2,1,0:T(2,128)(2,1)}), bf16[64,2,2048]{2,1,0:T(2,128)(2,1)S(1)}, u32[]{:S(2)}, u32[]{:S(2)}) async-start(bf16[64,2,2048]{2,1,0:T(2,128)(2,1)} %reshape.296), calls=%async_computation.1 | async-start | bytes 1048576 | tf_op jit(solution)/shard_map/all_to_all | solution.py:32
  57.9 57.6 %all-to-all-start.2 = ((bf16[128,2,8,512]{3,2,1,0:T(8,128)(2,1)}), bf16[128,2,8,512]{3,2,1,0:T(8,128)(2,1)}, u32[]{:S(2)}, u32[]{:S(2)}) async-start(bf16[128,2,8,512]{3,2,1,0:T(8,128)(2,1)} %copy.58), calls=%async_computation.2 | async-start | bytes 4194304 | tf_op jit(solution)/shard_map/all_to_all | solution.py:44
  115.5 4.7 %copy-start = (f32[1,2,512,512]{2,3,1,0:T(8,128)S(1)}, f32[1,2,512,512]{2,3,1,0:T(8,128)}, u32[]{:S(2)}) copy-start(f32[1,2,512,512]{2,3,1,0:T(8,128)} %copy.80) | copy-start | bytes 6291460
  120.3 1.2 copy-start.1
  120.3 1.5 copy-start.2
  193.3 26.8 %copy-start.3 = (bf16[128,2048]{1,0:T(8,128)(2,1)S(1)}, bf16[128,2048]{1,0:T(8,128)(2,1)}, u32[]{:S(2)}) copy-start(bf16[128,2048]{1,0:T(8,128)(2,1)} %param.5) | copy-start | bytes 1572868
  216.7 12.7 %all-to-all-start.5 = ((bf16[4,128,512]{2,1,0:T(8,128)(2,1)}), bf16[4,128,512]{2,1,0:T(8,128)(2,1)S(1)}, u32[]{:S(2)}, u32[]{:S(2)}) async-start(bf16[4,128,512]{2,1,0:T(8,128)(2,1)} %bitcast.30), calls=%async_computation.5 | async-start | bytes 1048576 | tf_op jit(solution)/shard_map/all_to_all | solution.py:68
  220.4 9.4 %copy-start.4 = (f32[2048]{0:T(1024)S(1)}, f32[2048]{0:T(1024)}, u32[]{:S(2)}) copy-start(f32[2048]{0:T(1024)} %param.9) | copy-start | bytes 24580
where the time goes:
time: 232 us; the launch traced here: 231 us
  blocking collectives  93.5 us (40%)
  waiting for transfers between devices  57.6 us (25%)
  local copies, waits for them, and re-layouts  30.7 us (13%)
  starting transfers between devices  23.3 us (10%)
  other arithmetic  17.6 us (8%)
  matrix products  8.25 us (4%)
    all_to_all x1, blocking collectives, convolve(): lax.all_to_all(back.astype(bf16), 'seq', split_axis=2, concat_axis=0, til...  57.1 us
    all_to_all x1, waiting for transfers between devices, convolve(): lax.all_to_all(part.astype(bf16), 'seq', split_axis=0, concat_axis=2, til...  31.6 us
    all_to_all x1, blocking collectives, convolve(): lax.all_to_all(field.astype(bf16), 'seq', split_axis=0, concat_axis=1, ti...  23 us
    all_to_all x1, waiting for transfers between devices, convolve(): lax.all_to_all(product.reshape(1, tokens, width), 'seq', split_axis=1, co...  17 us
    all_to_all x1, blocking collectives, per_device(): lax.all_to_all(product, 'ch', split_axis=1, concat_axis=0, tiled=True)  13.4 us
    all_to_all x1, starting transfers between devices, convolve(): lax.all_to_all(product.reshape(1, tokens, width), 'seq', split_axis=1, co...  13.3 us
    another operation x6, other arithmetic  11 us
    unnamed x19, local copies, waits for them, and re-layouts  10.2 us
  transfers between devices with their start and end apart: 3, of which 3 were waited for; matrix products, arithmetic and copies ran while one was open for 9% of the time, Pallas kernels for 0%

commit v1 on v0

--- a/solution.py
+++ b/solution.py
@@ -19,6 +19,14 @@
 
 
 def convolve(product, spectrum):
+
+    def wrap_layers_all_in(v0):
+        local_next = lax.all_to_all(
+            jnp.stack(jnp.split(v0, lax.axis_size("seq"), axis=2), axis=0), "seq", 0, 0
+        )
+        passed = jnp.concatenate(local_next, axis=0)
+        return passed
+
     seq_count = lax.axis_size("seq")
     tokens, width = product.shape
     length_two = 2 * seq_count * tokens
@@ -55,7 +63,7 @@
     back = jnp.stack(
         [back[:, 0] * un_cos - back[:, 1] * un_sin, back[:, 1] * un_cos + back[:, 0] * un_sin], 1
     )
-    back = lax.all_to_all(back.astype(bf16), "seq", split_axis=2, concat_axis=0, tiled=True)
+    back = wrap_layers_all_in(back.astype(bf16))
     field = dot("kip,kirc->prc", off, back) / length_two
     field = lax.all_to_all(field.astype(bf16), "seq", split_axis=0, concat_axis=1, tiled=True)
     return field.reshape(tokens, width)

time: 232 us -> 223 us (0.961)
  local copies, waits for them, and re-layouts: 30.7 us -> 20 us
    all_to_all x3 -> x0, local copies, waits for them, and re-layouts: 6.65 us -> none  [convolve(): lax.all_to_all(back.astype(bf16), 'seq', split_axis=2, concat_axis=0, til...]
    another operation x1 -> x0, local copies, waits for them, and re-layouts: 4.04 us -> none  [convolve(): jnp.stack([back[:, 0] * un_cos - back[:, 1] * un_sin, back[:, 1] * un_cos...]
where the time goes in v1:
time: 223 us
  blocking collectives  93.3 us (42%)
  waiting for transfers between devices  57.6 us (26%)
  starting transfers between devices  23.3 us (10%)
  local copies, waits for them, and re-layouts  20 us (9%)
  other arithmetic  17.5 us (8%)
  matrix products  10.3 us (5%)
    all_to_all x1, blocking collectives, wrap_layers_all_in(): lax.all_to_all(jnp.stack(jnp.split(v0, lax.axis_size('seq'), axis=2), axi...  56.9 us
    all_to_all x1, waiting for transfers between devices, convolve(): lax.all_to_all(part.astype(bf16), 'seq', split_axis=0, concat_axis=2, til...  31.6 us
    all_to_all x1, blocking collectives, convolve(): lax.all_to_all(field.astype(bf16), 'seq', split_axis=0, concat_axis=1, ti...  23 us
    all_to_all x1, waiting for transfers between devices, convolve(): lax.all_to_all(product.reshape(1, tokens, width), 'seq', split_axis=1, co...  17 us
    all_to_all x1, blocking collectives, per_device(): lax.all_to_all(product, 'ch', split_axis=1, concat_axis=0, tiled=True)  13.4 us
    all_to_all x1, starting transfers between devices, convolve(): lax.all_to_all(product.reshape(1, tokens, width), 'seq', split_axis=1, co...  13.3 us
    another operation x6, other arithmetic  10.8 us
    dot_general x4, matrix products, dot(): jnp.einsum(eq, a.astype(bf16), b.astype(bf16), preferred_element_type=f32)  10.3 us
  transfers between devices with their start and end apart: 3, of which 3 were waited for; matrix products, arithmetic and copies ran while one was open for 9% of the time, Pallas kernels for 0%

profile of v1, /device:TPU:1, one launch (start us, length us, event | category | flops | bytes accessed | tf_op | source)
XLA Modules:
  0.0 222.8 jit_solution(7081471842509237084)
XLA Ops:
  0.0 1.3 copy.53
  1.3 1.3 copy.54
  2.8 13.4 %all_to_all.73 = bf16[128,4,512]{0,2,1:T(8,128)(2,1)S(1)} all-to-all(bf16[128,4,512]{0,2,1:T(8,128)(2,1)S(1)} %bitcast.223), channel_id=1, replica_groups=mesh['seq'=64,'ch'=4] {'ch'}, dimensions={1} | all-to-all | bytes 1048576 | tf_op jit(solution)/shard_map/all_to_all | solution.py:74
  16.4 0.8 copy.104
  17.2 0.5 broadcast.368
  17.7 3.8 %reduce = bf16[512,512]{1,0:T(8,128)(2,1)S(1)} reduce(bf16[512,1,512]{2,1,0:T(2,128)(2,1)S(1)} %bitcast.225, bf16[]{:T(256)} %broadcast.368), dimensions={1}, to_apply=%bitcast.222.reduce_sub_computation | reduce | bytes 1048578
  21.5 1.0 reshape.300
  22.5 13.3 %all-to-all-start.1 = ((bf16[64,2,2048]{2,1,0:T(2,128)(2,1)}), bf16[64,2,2048]{2,1,0:T(2,128)(2,1)S(1)}, u32[]{:S(2)}, u32[]{:S(2)}) async-start(bf16[64,2,2048]{2,1,0:T(2,128)(2,1)} %reshape.300), calls=%async_computation.1 | async-start | bytes 1048576 | tf_op jit(solution)/shard_map/all_to_all | solution.py:40
  36.2 17.0 %all-to-all-done.1 = bf16[64,2,2048]{2,1,0:T(2,128)(2,1)S(1)} async-done(((bf16[64,2,2048]{2,1,0:T(2,128)(2,1)}), bf16[64,2,2048]{2,1,0:T(2,128)(2,1)S(1)}, u32[]{:S(2)}, u32[]{:S(2)}) %all-to-all-start.1) | async-done | bytes 524320 | tf_op jit(solution)/shard_map/all_to_all | solution.py:40
  53.2 0.5 reshape.301
  53.9 0.7 fusion.29
  54.6 0.6 add_convert_fusion.1
  55.4 2.5 %copy.58 = bf16[128,2,8,512]{3,2,1,0:T(8,128)(2,1)} copy(bf16[128,2,8,512]{3,0,2,1:T(8,128)(2,1)S(1)} %pad_maximum_fusion) | data formatting | bytes 4194304 | tf_op jit(solution)/shard_map/stack | solution.py:49
  57.9 6.5 %all-to-all-start.2 = ((bf16[128,2,8,512]{3,2,1,0:T(8,128)(2,1)}), bf16[128,2,8,512]{3,2,1,0:T(8,128)(2,1)}, u32[]{:S(2)}, u32[]{:S(2)}) async-start(bf16[128,2,8,512]{3,2,1,0:T(8,128)(2,1)} %copy.58), calls=%async_computation.2 | async-start | bytes 4194304 | tf_op jit(solution)/shard_map/all_to_all | solution.py:52
  64.4 4.6 %fusion.123 = (f32[1,2,512,512]{3,2,1,0:T(8,128)}, f32[1,2,512,512]{3,2,1,0:T(8,128)}) fusion(f32[2,2,512,512]{3,2,1,0:T(8,128)} %param.8), kind=kLoop, calls=%fused_computation.345 | loop fusion | bytes 8388608 | tf_op jit(solution)/shard_map/slice | solution.py:56
  69.0 1.9 copy.83
  71.0 2.9 %copy.84 = f32[1,2,512,512]{2,3,1,0:T(8,128)} copy(f32[1,2,512,512]{3,2,1,0:T(8,128)} %get-tuple-element.12) | data formatting | bytes 4194304
  73.9 4.0 %fusion.33 = bf16[1,512,512]{2,1,0:T(8,128)(2,1)S(1)} fusion(), kind=kLoop, calls=%fused_computation.176 | loop fusion | flops 3932160 | bytes 524288 | tf_op jit(solution)/shard_map/convert.13
  77.8 4.3 %negate_convert_fusion = (bf16[1,512,512]{2,1,0:T(8,128)(2,1)S(1)}, bf16[1,512,512]{2,1,0:T(8,128)(2,1)S(1)}) fusion(), kind=kLoop, calls=%fused_computation.165 | loop fusion | flops 4456448 | bytes 1048576 | tf_op jit(solution)/shard_map/convert.9
  82.2 1.5 maximum_bitcast_fusion.3
  83.9 31.6 %all-to-all-done.2 = bf16[128,2,8,512]{3,2,1,0:T(8,128)(2,1)} async-done(((bf16[128,2,8,512]{3,2,1,0:T(8,128)(2,1)}), bf16[128,2,8,512]{3,2,1,0:T(8,128)(2,1)}, u32[]{:S(2)}, u32[]{:S(2)}) %all-to-all-start.2) | async-done | bytes 2097184 | tf_op jit(solution)/shard_map/all_to_all | solution.py:52
  115.5 4.7 %convolution_bitcast_fusion.1 = f32[2,2,512,512]{2,3,1,0:T(8,128)S(1)} fusion(bf16[2,2,64,8,512]{4,3,1,0,2:T(8,128)(2,1)} %bitcast.7, bf16[1,2,512,512]{3,2,1,0:T(8,128)(2,1)} %get-tuple-element.14, bf16[1,2,512,512]{3,2,1,0:T(8,128)(2,1)} %get-tuple-element.13), kind=kOutput, calls=%fused_computation.127 | convolution fusion | flops 2151677952 | bytes 8388608 | tf_op jit(solution)/shard_map/oisr,girc->gosc/dot_general | solution.py:18
  120.3 1.2 fusion.6
  121.8 2.5 %convolution_bitcast_fusion = f32[2,2,512,512]{3,2,1,0:T(8,128)S(1)} fusion(bf16[2,1,512,512]{2,3,1,0:T(8,128)(2,1)S(1)} %get-tuple-element.6, bf16[2,1,512,512]{2,3,1,0:T(8,128)(2,1)S(1)} %get-tuple-element.5, bf16[1,2,512,512]{3,2,1,0:T(8,128)(2,1)S(1)} %copy-done.2, bf16[1,2,512,512]{3,2,1,0:T(8,128)(2,1)S(1)} %copy-done.1), kind=kOutput, calls=%fused_computation.126 | convolution fusion | flops 2155872256 | bytes 8388608 | tf_op jit(solution)/shard_map/oisr,gosc->girc/dot_general | solution.py:18
  124.3 0.6 subtract_convert_fusion
  125.6 56.9 %all_to_all.74 = bf16[64,2,2,8,512]{4,3,2,1,0:T(8,128)(2,1)S(1)} all-to-all(bf16[64,2,2,8,512]{4,3,2,1,0:T(8,128)(2,1)S(1)} %constant_dynamic-update-slice_fusion), channel_id=1, replica_groups=mesh['seq'=64,'ch'=4] {'seq'}, dimensions={0} | all-to-all | bytes 4194304 | tf_op jit(solution)/shard_map/all_to_all | solution.py:24
  182.5 2.4 %fusion.18 = bf16[64,8,512]{2,0,1:T(8,128)(2,1)S(1)} fusion(bf16[128,2,8,512]{3,2,1,0:T(8,128)(2,1)S(1)} %bitcast.228, bf16[128,1,64]{0,2,1:T(8,128)(2,1)S(1)} %get-tuple-element.19, bf16[128,1,64]{0,2,1:T(8,128)(2,1)S(1)} %get-tuple-element.20), kind=kOutput, calls=%fused_computation.155 | convolution fusion | flops 134807552 | bytes 2654208 | tf_op jit(solution)/shard_map/kip,kirc->prc/dot_general | solution.py:18
  185.2 23.0 %all_to_all.75 = bf16[64,8,512]{2,1,0:T(8,128)(2,1)} all-to-all(bf16[64,8,512]{2,1,0:T(8,128)(2,1)S(1)} %copy.66), channel_id=1, replica_groups=mesh['seq'=64,'ch'=4] {'seq'}, dimensions={0} | all-to-all | bytes 1048576 | tf_op jit(solution)/shard_map/all_to_all | solution.py:68
  208.3 3.5 %all-to-all-start.5 = ((bf16[4,128,512]{2,1,0:T(8,128)(2,1)}), bf16[4,128,512]{2,1,0:T(8,128)(2,1)S(1)}, u32[]{:S(2)}, u32[]{:S(2)}) async-start(bf16[4,128,512]{2,1,0:T(8,128)(2,1)} %bitcast.92), calls=%async_computation.5 | async-start | bytes 1048576 | tf_op jit(solution)/shard_map/all_to_all | solution.py:76
  212.0 9.0 %all-to-all-done.5 = bf16[4,128,512]{2,1,0:T(8,128)(2,1)S(1)} async-done(((bf16[4,128,512]{2,1,0:T(8,128)(2,1)}), bf16[4,128,512]{2,1,0:T(8,128)(2,1)S(1)}, u32[]{:S(2)}, u32[]{:S(2)}) %all-to-all-start.5) | async-done | bytes 524320 | tf_op jit(solution)/shard_map/all_to_all | solution.py:76
  221.5 0.3 fusion.25
  221.8 1.0 copy.68
  (87 shorter events, 2.7 us)
Async XLA Ops:
  22.5 30.7 %all-to-all-start.1 = ((bf16[64,2,2048]{2,1,0:T(2,128)(2,1)}), bf16[64,2,2048]{2,1,0:T(2,128)(2,1)S(1)}, u32[]{:S(2)}, u32[]{:S(2)}) async-start(bf16[64,2,2048]{2,1,0:T(2,128)(2,1)} %reshape.300), calls=%async_computation.1 | async-start | bytes 1048576 | tf_op jit(solution)/shard_map/all_to_all | solution.py:40
  57.9 57.6 %all-to-all-start.2 = ((bf16[128,2,8,512]{3,2,1,0:T(8,128)(2,1)}), bf16[128,2,8,512]{3,2,1,0:T(8,128)(2,1)}, u32[]{:S(2)}, u32[]{:S(2)}) async-start(bf16[128,2,8,512]{3,2,1,0:T(8,128)(2,1)} %copy.58), calls=%async_computation.2 | async-start | bytes 4194304 | tf_op jit(solution)/shard_map/all_to_all | solution.py:52
  115.5 4.7 %copy-start = (f32[1,2,512,512]{2,3,1,0:T(8,128)S(1)}, f32[1,2,512,512]{2,3,1,0:T(8,128)}, u32[]{:S(2)}) copy-start(f32[1,2,512,512]{2,3,1,0:T(8,128)} %copy.84) | copy-start | bytes 6291460
  120.3 1.2 copy-start.1
  120.3 1.5 copy-start.2
  184.9 26.8 %copy-start.3 = (bf16[128,2048]{1,0:T(8,128)(2,1)S(1)}, bf16[128,2048]{1,0:T(8,128)(2,1)}, u32[]{:S(2)}) copy-start(bf16[128,2048]{1,0:T(8,128)(2,1)} %param.5) | copy-start | bytes 1572868
  208.3 12.7 %all-to-all-start.5 = ((bf16[4,128,512]{2,1,0:T(8,128)(2,1)}), bf16[4,128,512]{2,1,0:T(8,128)(2,1)S(1)}, u32[]{:S(2)}, u32[]{:S(2)}) async-start(bf16[4,128,512]{2,1,0:T(8,128)(2,1)} %bitcast.92), calls=%async_computation.5 | async-start | bytes 1048576 | tf_op jit(solution)/shard_map/all_to_all | solution.py:76
  212.0 9.4 %copy-start.4 = (f32[2048]{0:T(1024)S(1)}, f32[2048]{0:T(1024)}, u32[]{:S(2)}) copy-start(f32[2048]{0:T(1024)} %param.9) | copy-start | bytes 24580
